TPU v7x, 256 devices: a whole 4x4x8 slice. The times are simulated.
256 devices in a mesh: expert: 32 (over y, x, core), group: 8 (over z).
Axes of the slice: x: 4, y: 4, z: 8, core: 2. Of those that a mesh axis runs over, the one named last changes fastest.
Arguments:
- activations: bfloat16 [4096, 7168], P('expert', 'group'), may hold values from -6 to 6
- out_grads: bfloat16 [4096, 7168], P('expert', 'group'), may hold values from -6 to 6
- sketch_op: bfloat16 [7168, 128], P('group'), may hold values from -0.0625 to 0.0625
- block_lists: int32 [256, 32], P('expert'), may hold values from 0 to 31, as said below
- block_counts: int32 [256], P('expert'), may hold values from 1 to 32
- gate_values: bfloat16 [256, 32, 128], P('expert'), may hold values from 0.05 to 9, as said below
Outputs:
- basis_out: float32 [256, 7168, 128], P('expert', 'group')
Inputs may be any that keep to these rules, and one draw needn't show every extreme that they name: `block_lists`: each row is an ordering of all 32 block numbers, each once. `gate_values`: positive.
All inputs are finite; a program needn't handle non-finite values.
Results may differ from a plain program's by a relative error of at most 0.0042.
The roundings to bfloat16 on the way count: a program that leaves them out, or rounds other values in their place, can miss the bound.
Values may be sent and summed in bfloat16 or wider, within the bound.
No kernel may reach another device: no remote copies, remote signals or barrier semaphores. Data moves between devices by JAX's collectives and lax.ppermute only.
A program may use at most 64 MiB of HBM per device.

v0:
```python
import math
import jax
import jax.numpy as jnp
from jax import lax
from jax.sharding import PartitionSpec as P


def sketch_rows(rows_x, rows_y, weight_part):
    count_exp = weight_part.shape[0]
    row_count = rows_x.shape[0]
    sketch_rank = rows_y.shape[1]
    rows_wide = rows_y.astype(jnp.float32)
    contract = (((0,), (0,)), ((), ()))
    scaled = (weight_part.T[:, :, None] * rows_wide[:, None, :]).astype(jnp.bfloat16)
    scaled = scaled.reshape(row_count, count_exp * sketch_rank)
    return lax.dot_general(rows_x, scaled, contract, preferred_element_type=jnp.float32)


def gram_of(sketch_flat, sketch_rank):
    shaped = sketch_flat.reshape(sketch_flat.shape[0], -1, sketch_rank)
    return jnp.einsum("dkr,dks->rs", shaped, shaped, precision=lax.Precision.HIGHEST)


def on_device(activations, out_grads, sketch_op, block_lists, block_counts, gate_values):
    sketch_rank = sketch_op.shape[1]
    feat_width = activations.shape[1]
    local_exp = block_lists.shape[0]
    blocks = block_lists.shape[1]
    partial_sketch = jnp.dot(out_grads, sketch_op, preferred_element_type=jnp.float32)
    sketched = lax.psum(partial_sketch, "group").astype(jnp.bfloat16)
    slot_ids = jnp.arange(blocks, dtype=jnp.int32)
    slot_live = slot_ids[None, :] < block_counts[:, None]
    onehot = ((block_lists[:, :, None] == slot_ids[None, None, :]) & slot_live[:, :, None]).astype(
        jnp.float32
    )
    weights = jnp.einsum("ejb,ejt->ebt", onehot, gate_values.astype(jnp.float32)).reshape(
        local_exp, -1
    )
    piece_rows = lax.all_gather(activations, "expert", axis=0, tiled=True)
    piece_sketch = lax.all_gather(sketched, "expert", axis=0, tiled=True)
    sketch_all = sketch_rows(piece_rows, piece_sketch, weights)
    gram_total = lax.psum(gram_of(sketch_all, sketch_rank), ("expert", "group"))
    factor = jnp.linalg.cholesky(gram_total)
    stacked = (
        sketch_all.reshape(feat_width, local_exp, sketch_rank)
        .transpose(1, 0, 2)
        .reshape(-1, sketch_rank)
    )
    basis_flat = lax.linalg.triangular_solve(
        factor, stacked, left_side=False, lower=True, transpose_a=True
    )
    out_scale = math.sqrt(local_exp * lax.axis_size("expert") * feat_width * lax.axis_size("group"))
    return (basis_flat * out_scale).reshape(local_exp, feat_width, sketch_rank)


def solution(mesh):
    in_specs = (
        P("expert", "group"),
        P("expert", "group"),
        P("group", None),
        P("expert", None),
        P("expert"),
        P("expert", None, None),
    )
    out_specs = P("expert", "group", None)
    return jax.shard_map(
        on_device, mesh=mesh, in_specs=in_specs, out_specs=out_specs, check_vma=False
    )
```

profile of v0, /device:TPU:1, one launch (start us, length us, event | category | flops | bytes accessed | tf_op | source)
XLA Modules:
  0.0 443.5 jit_solution(5734964180359648877)
XLA Ops:
  6.5 0.0 copy-start
  6.5 0.0 all-gather.3.cloned.1.call-start
  6.5 0.9 copy-done
  7.5 1.1 fusion.10
  8.6 27.5 %psum.14 = bf16[128,128]{1,0:T(8,128)(2,1)} all-reduce(f32[128,128]{1,0:T(8,128)S(1)} %fusion.10), channel_id=1, replica_groups=mesh['expert'=32,'group'=8] {'group'}, use_global_device_ids=true, to_apply=%region_0.0 | all-reduce | flops 16384 | bytes 98304 | tf_op jit(solution)/shard_map/psum | solution.py:30
  36.2 0.0 all-gather.3.cloned.1.call-update
  36.2 0.0 all-gather.5.cloned.1.call-start
  36.2 0.7 all-gather.5.cloned.1.call-update
  36.9 0.0 all-reduce.2.cloned.1.call-start
  37.0 0.7 iota_compare_fusion.3
  37.7 1.0 convolution_bitcast_fusion
  38.7 0.1 copy.26
  38.8 0.6 copy.11
  39.4 50.1 %all-gather.3.cloned.1.call-done = bf16[4096,128]{1,0:T(8,128)(2,1)} async-done(((bf16[128,128]{1,0:T(8,128)(2,1)}), bf16[4096,128]{1,0:T(8,128)(2,1)}) %all-gather.3.cloned.1.call-update) | async-done | bytes 1048592 | tf_op jit(solution)/shard_map/all_gather | solution.py:40
  89.5 1.4 convert_element_type.16
  90.9 16.4 %multiply_convert_fusion = bf16[4096,8,128]{2,1,0:T(8,128)(2,1)} fusion(f32[4096,128]{1,0:T(8,128)S(1)} %convert_element_type.16, f32[4096,8]{1,0:T(8,128)S(1)} %copy.11), kind=kLoop, calls=%fused_computation | loop fusion | flops 8388608 | bytes 10616832 | tf_op jit(solution)/shard_map/convert_element_type | solution.py:14
  107.2 40.0 %all-gather.5.cloned.1.call-done = bf16[4096,896]{1,0:T(8,128)(2,1)} async-done(((bf16[128,896]{1,0:T(8,128)(2,1)}), bf16[4096,896]{1,0:T(8,128)(2,1)}) %all-gather.5.cloned.1.call-update) | async-done | bytes 7340048 | tf_op jit(solution)/shard_map/all_gather | solution.py:39
  147.3 12.9 %fusion = f32[1024,896]{1,0:T(8,128)S(1)} fusion(bf16[4096,896]{1,0:T(8,128)(2,1)} %all-gather.5.cloned.1.call-done, bf16[512,8,8,128]{3,2,1,0:T(8,128)(2,1)} %bitcast.40), kind=kOutput, calls=%fused_computation.2 | convolution fusion | flops 7516192768 | bytes 19398656 | tf_op jit(solution)/shard_map/dot_general | solution.py:16
  160.2 0.0 copy-start.1
  160.2 1.8 copy-done.1
  162.1 3.6 convolution_bitcast_fusion.1
  165.7 0.0 all-reduce.2.cloned.1.call-update
  165.7 5.0 %copy.12 = f32[896,8,128]{2,0,1:T(8,128)} copy(f32[896,8,128]{0,2,1:T(8,128)} %bitcast.38) | data formatting | bytes 7340032 | tf_op jit(solution)/shard_map/reshape | solution.py:45
  170.7 235.7 %all-reduce.2.cloned.1.call-done = f32[128,128]{0,1:T(8,128)} async-done(((f32[128,128]{0,1:T(8,128)}), f32[128,128]{0,1:T(8,128)}) %all-reduce.2.cloned.1.call-update) | async-done | bytes 65552 | tf_op jit(solution)/shard_map/psum | solution.py:42
  406.4 0.9 copy.15
  407.4 0.9 fusion.7
  408.2 11.7 %cholesky.16 = f32[128,128]{1,0:T(8,128)S(1)} custom-call(f32[128,128]{1,0:T(8,128)S(1)} %fusion.7), custom_call_target="Cholesky" | custom-call | tf_op jit(solution)/shard_map/jit(cholesky)/cholesky | solution.py:43
  420.0 0.6 compare_reduce_fusion
  420.6 0.7 fusion.5
  421.3 9.8 %custom-call.6 = f32[1,128,128]{1,2,0:T(8,128)S(1)} custom-call(f32[1,128,128]{2,1,0:T(8,128)S(1)} %fusion.5), custom_call_target="InvertDiagBlocksLowerTriangular" | custom-call | tf_op jit(solution)/shard_map/triangular_solve | solution.py:49
  431.1 5.9 %convolution_multiply_fusion = f32[7168,128]{1,0:T(8,128)} fusion(f32[7168,128]{1,0:T(8,128)} %bitcast.39, f32[1,128,128]{1,2,0:T(8,128)S(1)} %custom-call.6), kind=kOutput, calls=%fused_computation.1 | convolution fusion | flops 1410203648 | bytes 7405568 | tf_op jit(solution)/shard_map/triangular_solve | solution.py:49
  (1 shorter events, 0.0 us)
Async XLA Ops:
  6.5 0.9 copy-start
  6.5 83.0 %all-gather.3.cloned.1.call-start = ((), (), s32[]{:S(2)}) async-start(), calls=%async_computation | async-start | bytes 1081344 | tf_op jit(solution)/shard_map/all_gather | solution.py:40
  36.2 111.1 %all-gather.5.cloned.1.call-start = ((), (), s32[]{:S(2)}) async-start(), calls=%async_computation.1 | async-start | bytes 7569408 | tf_op jit(solution)/shard_map/all_gather | solution.py:39
  36.9 369.5 %all-reduce.2.cloned.1.call-start = ((), (), s32[]{:S(2)}) async-start(), calls=%async_computation.2 | async-start | bytes 131072 | tf_op jit(solution)/shard_map/psum | solution.py:42
  160.2 1.8 copy-start.1
Sparse Core Ops, SparseCore 0:
  36.3 53.1 all-gather.2
  92.0 55.1 all-gather.4
  165.8 240.5 all-reduce.1
where the time goes:
time: 444 us
  waiting for transfers between devices  327 us (74%)
  other arithmetic  42.2 us (10%)
  blocking collectives  27.5 us (6%)
  matrix products  24.7 us (6%)
  between operations  13.2 us (3%)
  local copies, waits for them, and re-layouts  9.39 us (2%)
    psum x1, waiting for transfers between devices, on_device(): gram_total = lax.psum(gram_of(sketch_all, sketch_rank), ('expert', 'group'))  236 us
    all_gather x1, waiting for transfers between devices, on_device(): piece_sketch = lax.all_gather(sketched, 'expert', axis=0, tiled=True)  50.1 us
    all_gather x1, waiting for transfers between devices, on_device(): piece_rows = lax.all_gather(activations, 'expert', axis=0, tiled=True)  40 us
    psum x1, blocking collectives, on_device(): sketched = lax.psum(partial_sketch, 'group').astype(jnp.bfloat16)  27.5 us
    convert_element_type x1, other arithmetic, sketch_rows(): (weight_part.T[:, :, None] * rows_wide[:, None, :]).astype(jnp.bfloat16)  16.4 us
    dot_general x1, matrix products, sketch_rows(): lax.dot_general(rows_x, scaled, contract, preferred_element_type=jnp.floa...  12.9 us
    another operation x3, other arithmetic, on_device(): factor = jnp.linalg.cholesky(gram_total)  12.4 us
    another operation x2, other arithmetic, on_device(): lax.linalg.triangular_solve(factor, stacked, left_side=False, lower=True,...  10.5 us
  transfers between devices with their start and end apart: 3, of which 3 were waited for; matrix products, arithmetic and copies ran while one was open for 6% of the time, Pallas kernels for 0%

commit v1 on v0

--- a/solution.py
+++ b/solution.py
@@ -39,7 +39,9 @@
     piece_rows = lax.all_gather(activations, "expert", axis=0, tiled=True)
     piece_sketch = lax.all_gather(sketched, "expert", axis=0, tiled=True)
     sketch_all = sketch_rows(piece_rows, piece_sketch, weights)
-    gram_total = lax.psum(gram_of(sketch_all, sketch_rank), ("expert", "group"))
+    gram_total = jnp.sum(
+        lax.all_gather(gram_of(sketch_all, sketch_rank), ("expert", "group")), axis=0
+    )
     factor = jnp.linalg.cholesky(gram_total)
     stacked = (
         sketch_all.reshape(feat_width, local_exp, sketch_rank)

time: 444 us -> 333 us (0.75)
  waiting for transfers between devices: 327 us -> 210 us
  other arithmetic: 42.2 us -> 47.9 us
    psum x1 -> x0, waiting for transfers between devices: 236 us -> none  [on_device(): gram_total = lax.psum(gram_of(sketch_all, sketch_rank), ('expert', 'group'))]
    all_gather x0 -> x1, waiting for transfers between devices: none -> 120 us  [on_device(): lax.all_gather(gram_of(sketch_all, sketch_rank), ('expert', 'group'))]
    reduce_sum x0 -> x1, other arithmetic: none -> 6.59 us  [on_device(): jnp.sum(lax.all_gather(gram_of(sketch_all, sketch_rank), ('expert', 'grou...]
  transfers between devices with their start and end apart: 3 -> 3, of which waited for: 3 -> 3; matrix products, arithmetic and copies ran while one was open for 6% -> 8% of each run, Pallas kernels for 0% -> 0%
where the time goes in v1:
time: 333 us; the launch traced here: 332 us
  waiting for transfers between devices  210 us (63%)
  other arithmetic  47.9 us (14%)
  blocking collectives  27.5 us (8%)
  matrix products  24.6 us (7%)
  between operations  13.2 us (4%)
  local copies, waits for them, and re-layouts  8.55 us (3%)
    all_gather x1, waiting for transfers between devices, on_device(): lax.all_gather(gram_of(sketch_all, sketch_rank), ('expert', 'group'))  120 us
    all_gather x1, waiting for transfers between devices, on_device(): piece_sketch = lax.all_gather(sketched, 'expert', axis=0, tiled=True)  50.1 us
    all_gather x1, waiting for transfers between devices, on_device(): piece_rows = lax.all_gather(activations, 'expert', axis=0, tiled=True)  40 us
    psum x1, blocking collectives, on_device(): sketched = lax.psum(partial_sketch, 'group').astype(jnp.bfloat16)  27.5 us
    convert_element_type x1, other arithmetic, sketch_rows(): (weight_part.T[:, :, None] * rows_wide[:, None, :]).astype(jnp.bfloat16)  16.4 us
    dot_general x1, matrix products, sketch_rows(): lax.dot_general(rows_x, scaled, contract, preferred_element_type=jnp.floa...  12.9 us
    another operation x3, other arithmetic, on_device(): factor = jnp.linalg.cholesky(gram_total)  12.4 us
    another operation x2, other arithmetic, on_device(): lax.linalg.triangular_solve(factor, stacked, left_side=False, lower=True,...  10.5 us
  transfers between devices with their start and end apart: 3, of which 3 were waited for; matrix products, arithmetic and copies ran while one was open for 8% of the time, Pallas kernels for 0%

profile of v1, /device:TPU:1, one launch (start us, length us, event | category | flops | bytes accessed | tf_op | source)
XLA Modules:
  0.0 332.3 jit_solution(6978671600779309800)
XLA Ops:
  6.5 0.0 copy-start
  6.5 0.0 all-gather.5.cloned.1.call-start
  6.5 0.9 copy-done
  7.5 1.1 fusion.10
  8.6 27.5 %psum.7 = bf16[128,128]{1,0:T(8,128)(2,1)} all-reduce(f32[128,128]{1,0:T(8,128)S(1)} %fusion.10), channel_id=1, replica_groups=mesh['expert'=32,'group'=8] {'group'}, use_global_device_ids=true, to_apply=%region_0.0 | all-reduce | flops 16384 | bytes 98304 | tf_op jit(solution)/shard_map/psum | solution.py:30
  36.2 0.0 all-gather.5.cloned.1.call-update
  36.2 0.0 all-gather.7.cloned.1.call-start
  36.2 0.7 all-gather.7.cloned.1.call-update
  36.9 0.0 all-gather.9.cloned.1.call-start
  37.0 0.7 iota_compare_fusion.3
  37.7 1.0 convolution_bitcast_fusion
  38.7 0.1 copy.26
  38.8 0.6 copy.14
  39.4 50.1 %all-gather.5.cloned.1.call-done = bf16[4096,128]{1,0:T(8,128)(2,1)} async-done(((bf16[128,128]{1,0:T(8,128)(2,1)}), bf16[4096,128]{1,0:T(8,128)(2,1)}) %all-gather.5.cloned.1.call-update) | async-done | bytes 1048592 | tf_op jit(solution)/shard_map/all_gather | solution.py:40
  89.5 1.4 convert_element_type.16
  90.9 16.4 %multiply_convert_fusion = bf16[4096,8,128]{2,1,0:T(8,128)(2,1)} fusion(f32[4096,128]{1,0:T(8,128)S(1)} %convert_element_type.16, f32[4096,8]{1,0:T(8,128)S(1)} %copy.14), kind=kLoop, calls=%fused_computation | loop fusion | flops 8388608 | bytes 10616832 | tf_op jit(solution)/shard_map/convert_element_type | solution.py:14
  107.2 40.0 %all-gather.7.cloned.1.call-done = bf16[4096,896]{1,0:T(8,128)(2,1)} async-done(((bf16[128,896]{1,0:T(8,128)(2,1)}), bf16[4096,896]{1,0:T(8,128)(2,1)}) %all-gather.7.cloned.1.call-update) | async-done | bytes 7340048 | tf_op jit(solution)/shard_map/all_gather | solution.py:39
  147.3 12.9 %fusion = f32[1024,896]{1,0:T(8,128)S(1)} fusion(bf16[4096,896]{1,0:T(8,128)(2,1)} %all-gather.7.cloned.1.call-done, bf16[512,8,8,128]{3,2,1,0:T(8,128)(2,1)} %bitcast.42), kind=kOutput, calls=%fused_computation.2 | convolution fusion | flops 7516192768 | bytes 19398656 | tf_op jit(solution)/shard_map/dot_general | solution.py:16
  160.2 0.0 copy-start.1
  160.2 1.8 copy-done.1
  162.1 3.6 %convolution_bitcast_fusion.1 = f32[128,128]{1,0:T(8,128)} fusion(f32[896,8,128]{0,2,1:T(8,128)S(1)} %bitcast.38), kind=kOutput, calls=%fused_computation.6 | convolution fusion | flops 1409286144 | bytes 3735552 | tf_op jit(solution)/shard_map/dkr,dks->rs/dot_general | solution.py:21
  165.7 0.0 all-gather.9.cloned.1.call-update
  165.7 5.0 %copy.15 = f32[896,8,128]{2,0,1:T(8,128)} copy(f32[896,8,128]{0,2,1:T(8,128)} %bitcast.39) | data formatting | bytes 7340032 | tf_op jit(solution)/shard_map/reshape | solution.py:47
  170.7 119.5 %all-gather.9.cloned.1.call-done = f32[32768,128]{1,0:T(8,128)} async-done(((f32[128,128]{1,0:T(8,128)}), f32[32768,128]{1,0:T(8,128)}) %all-gather.9.cloned.1.call-update) | async-done | bytes 16777232 | tf_op jit(solution)/shard_map/all_gather | solution.py:43
  290.3 6.6 %reduce_sum.9 = f32[128,128]{1,0:T(8,128)S(1)} reduce(f32[256,128,128]{2,1,0:T(8,128)} %bitcast.40, f32[]{:T(128)} %constant.39.clone.1), dimensions={0}, to_apply=%region_1.0 | reduce | flops 4177920 | bytes 16842756 | tf_op jit(solution)/shard_map/reduce_sum | solution.py:42
  296.8 0.1 copy.17
  297.0 11.7 %cholesky.16 = f32[128,128]{1,0:T(8,128)S(1)} custom-call(f32[128,128]{1,0:T(8,128)S(1)} %fusion.7), custom_call_target="Cholesky" | custom-call | tf_op jit(solution)/shard_map/jit(cholesky)/cholesky | solution.py:45
  308.7 0.6 compare_reduce_fusion
  309.3 0.7 fusion.5
  310.0 9.8 %custom-call.6 = f32[1,128,128]{1,2,0:T(8,128)S(1)} custom-call(f32[1,128,128]{2,1,0:T(8,128)S(1)} %fusion.5), custom_call_target="InvertDiagBlocksLowerTriangular" | custom-call | tf_op jit(solution)/shard_map/triangular_solve | solution.py:51
  319.8 5.9 %convolution_multiply_fusion = f32[7168,128]{1,0:T(8,128)} fusion(f32[7168,128]{1,0:T(8,128)} %bitcast.41, f32[1,128,128]{1,2,0:T(8,128)S(1)} %custom-call.6), kind=kOutput, calls=%fused_computation.1 | convolution fusion | flops 1410203648 | bytes 7405568 | tf_op jit(solution)/shard_map/triangular_solve | solution.py:51
  (2 shorter events, 0.0 us)
Async XLA Ops:
  6.5 0.9 copy-start
  6.5 83.0 %all-gather.5.cloned.1.call-start = ((), (), s32[]{:S(2)}) async-start(), calls=%async_computation | async-start | bytes 1081344 | tf_op jit(solution)/shard_map/all_gather | solution.py:40
  36.2 111.1 %all-gather.7.cloned.1.call-start = ((), (), s32[]{:S(2)}) async-start(), calls=%async_computation.1 | async-start | bytes 7569408 | tf_op jit(solution)/shard_map/all_gather | solution.py:39
  36.9 253.3 %all-gather.9.cloned.1.call-start = ((), (), s32[]{:S(2)}) async-start(), calls=%async_computation.2 | async-start | bytes 16842752 | tf_op jit(solution)/shard_map/all_gather | solution.py:43
  160.2 1.8 copy-start.1
Sparse Core Ops, SparseCore 0:
  36.3 53.1 all-gather.4
  92.0 55.1 all-gather.6
  165.8 124.3 all-gather.8
